TPU v7x, 32 devices: a whole 2x2x4 slice. The times are simulated.
32 devices in a mesh: seq: 4 (over y, x), span: 4 (over z), kvg: 2 (over core).
Axes of the slice: x: 2, y: 2, z: 4, core: 2. Of those that a mesh axis runs over, the one named last changes fastest.
Arguments:
- query_rows: bfloat16 [8704, 1792], P(('seq', 'span'), 'kvg'), parts along dimension 0, may hold values from -256 to 256
- key_rows: bfloat16 [8704, 256], P(('seq', 'span'), 'kvg'), parts along dimension 0, may hold values from -6 to 6
- value_rows: bfloat16 [8704, 256], P(('seq', 'span'), 'kvg'), parts along dimension 0, may hold values from -6 to 6
- out_grad: bfloat16 [8704, 1792], P(('seq', 'span'), 'kvg'), parts along dimension 0, may hold values from -6 to 6
- ratios: int32 [16], P('seq'), parts along dimension 0, may hold values from 16 to 64, as said below
Outputs:
- attended: bfloat16 [8704, 1792], P(('seq', 'span'), 'kvg'), parts along dimension 0
- query_grad: bfloat16 [8704, 1792], P(('seq', 'span'), 'kvg'), parts along dimension 0
- key_grad: bfloat16 [8704, 256], P(('seq', 'span'), 'kvg'), parts along dimension 0
- value_grad: bfloat16 [8704, 256], P(('seq', 'span'), 'kvg'), parts along dimension 0
There are 4 independent parts, one for each index of `seq`. A program takes and returns all parts, laid end to end along the dimension named above; each array names one. Nothing has to cross between parts.
Inputs may be any that keep to these rules, and one draw needn't show every extreme that they name: `ratios`: every ratio is 16, 32 or 64, and some span of every sequence has 16.
All inputs are finite; a program needn't handle non-finite values.
Results may differ from a plain program's by a relative error of at most 0.0096.
Values may be sent and summed in bfloat16 or wider, within the bound.
A program may use at most 64 MiB of HBM per device.

v0:
```python
import functools
import math

import jax
import jax.numpy as jnp
from jax import lax
from jax.experimental import pallas as pl
from jax.experimental.pallas import tpu as pltpu
from jax.sharding import PartitionSpec as P

SPAN = 512
HD = 128
BMAX = 32
BLK = 256

SCALE = HD ** (-0.5)
SCALE_LOG2E = SCALE * math.log2(math.e)
FLOOR = -1e30

f32 = jnp.float32
bf16 = jnp.bfloat16


def nt(a, b):
    return lax.dot_general(a, b, (((1,), (1,)), ((), ())), preferred_element_type=f32)


def nn(a, b):
    return lax.dot_general(a, b, (((1,), (0,)), ((), ())), preferred_element_type=f32)


def interleave(blocks):
    waiting, active = list(blocks), []
    while waiting or active:
        if waiting:
            active.append(waiting.pop(0))
        active = [block for block in active if next(block, "end") != "end"]


def kernel(
    n, heads,
    ratios_ref, q_hbm, k_hbm, v_hbm, g_hbm,
    o_hbm, dq_hbm, dk_out, dv_out,
    q_s, g_s, k_s, v_s, kt_s, vt_s, kb_s, vb_s, kbt_s, vbt_s,
    e_s, ot_s, stat_s, bias_s, bbias_s, term_s, recv_s, dk_s, dv_s, o_s, dq_s,
    in_sem, q_sem, g_sem, qb_sem, gb_sem, o_sem, dq_sem, ob_sem, dqb_sem,
    kv_send, kv_recv, term_send, term_recv,
):
    me = lax.axis_index("span")
    chunks = SPAN // BLK
    last = heads * chunks
    nb = n * BMAX

    barrier = pltpu.get_barrier_semaphore()
    for step in range(1, n):
        pl.semaphore_signal(
            barrier, inc=1, device_id={"span": lax.rem(me + step, n)},
            device_id_type=pl.DeviceIdType.MESH,
        )

    def head_cols(h):
        return pl.ds(h * HD, HD)

    def head_rows(h):
        return pl.ds(h * SPAN, SPAN)

    def block_rows(b):
        return pl.ds(b * BLK, BLK)

    def q_copy(h):
        return pltpu.make_async_copy(
            q_hbm.at[pl.ds(0, SPAN), head_cols(h)], q_s.at[head_rows(h)], q_sem.at[h]
        )

    def g_copy(h):
        return pltpu.make_async_copy(
            g_hbm.at[pl.ds(0, SPAN), head_cols(h)], g_s.at[head_rows(h)], g_sem.at[h]
        )

    def tail_copy(src, dst, sem, h):
        return pltpu.make_async_copy(
            src.at[pl.ds(SPAN, BMAX), pl.ds(h * HD, HD)],
            dst.at[pl.ds(last * BLK + h * BMAX, BMAX)],
            sem.at[h],
        )

    k_copy = pltpu.make_async_copy(k_hbm.at[pl.ds(0, SPAN)], k_s, in_sem.at[0])
    v_copy = pltpu.make_async_copy(v_hbm.at[pl.ds(0, SPAN)], v_s, in_sem.at[1])
    mine = pl.ds(pl.multiple_of(me * BMAX, BMAX), BMAX)
    kb_copy = pltpu.make_async_copy(
        k_hbm.at[pl.ds(SPAN, BMAX)], kb_s.at[mine], in_sem.at[2]
    )
    vb_copy = pltpu.make_async_copy(
        v_hbm.at[pl.ds(SPAN, BMAX)], vb_s.at[mine], in_sem.at[3]
    )
    k_copy.start()
    v_copy.start()
    q_copy(0).start()
    kb_copy.start()
    vb_copy.start()
    for h in range(1, heads):
        q_copy(h).start()
    for h in range(heads):
        tail_copy(q_hbm, q_s, qb_sem, h).start()
    for h in range(heads):
        g_copy(h).start()
    for h in range(heads):
        tail_copy(g_hbm, g_s, gb_sem, h).start()

    own_ratio = ratios_ref[me]
    key_id = lax.broadcasted_iota(jnp.int32, (nb, BLK), 0)
    lane_slot = lax.rem(lax.broadcasted_iota(jnp.int32, (nb, BLK), 1), BMAX)
    key_slot = lax.rem(key_id, BMAX)
    key_span = key_id // BMAX
    key_ratio = jnp.zeros((nb, BLK), jnp.int32)
    for s in range(n):
        key_ratio = jnp.where(key_span == s, ratios_ref[s], key_ratio)
    live = (key_slot + 1) * key_ratio <= SPAN
    before = live & (key_span < me)
    bias_s[...] = jnp.where(before, 0.0, FLOOR)
    bbias_s[...] = jnp.where(
        before | (live & (key_span == me) & (key_slot <= lane_slot)), 0.0, FLOOR
    )
    term_s[...] = jnp.zeros_like(term_s)
    dk_s[...] = jnp.zeros_like(dk_s)
    dv_s[...] = jnp.zeros_like(dv_s)
    pad = BLK - heads * BMAX
    q_s[pl.ds(last * BLK + heads * BMAX, pad), :] = jnp.zeros((pad, HD), bf16)
    g_s[pl.ds(last * BLK + heads * BMAX, pad), :] = jnp.zeros((pad, HD), bf16)

    pl.semaphore_wait(barrier, n - 1)

    def kv_copies(step):
        peer = lax.rem(me + step, n)
        return [
            pltpu.make_async_remote_copy(
                src_ref=src.at[pl.ds(SPAN, BMAX)], dst_ref=dst.at[mine],
                send_sem=kv_send.at[i, step - 1], recv_sem=kv_recv.at[i, step - 1],
                device_id={"span": peer}, device_id_type=pl.DeviceIdType.MESH,
            )
            for i, (src, dst) in enumerate(((k_hbm, kb_s), (v_hbm, vb_s)))
        ]

    for step in range(1, n):
        for copy in kv_copies(step):
            copy.start()

    k_copy.wait()
    v_copy.wait()
    kt_s[...] = k_s[...].T
    vt_s[...] = v_s[...].T

    row = lax.broadcasted_iota(jnp.int32, (BLK, BLK), 0)
    col = lax.broadcasted_iota(jnp.int32, (BLK, BLK), 1)

    def own_scores(b, masks, wait=None):
        if wait is not None:
            wait()
        query = q_s[block_rows(b), :]
        scores = nt(k_s[pl.ds(0, len(masks) * BLK), :], query)
        scores = [scores[c * BLK : (c + 1) * BLK] for c in range(len(masks))]
        scores = [
            s if mask is None else jnp.where(mask, s, FLOOR)
            for s, mask in zip(scores, masks)
        ]
        yield
        top = functools.reduce(
            jnp.maximum, [jnp.max(s, axis=0, keepdims=True) for s in scores]
        )
        yield
        total = jnp.zeros((1, BLK), f32)
        parts = []
        for c, s in enumerate(scores):
            e = jnp.exp2((s - top) * SCALE_LOG2E)
            total = total + jnp.sum(e, axis=0, keepdims=True)
            parts.append(e.astype(bf16))
            e_s[b, pl.ds(c * BLK, BLK), :] = parts[-1]
        yield
        mixed = nn(vt_s[:, pl.ds(0, len(masks) * BLK)], jnp.concatenate(parts, 0))
        ot_s[b] = mixed
        stat_s[b, 0:1, :] = top
        stat_s[b, 1:2, :] = total

    reach = (lax.rem(col, BMAX) + 1) * own_ratio

    def tails_in(src, dst, sem):
        for h in range(heads):
            tail_copy(src, dst, sem, h).wait()

    interleave(
        [
            own_scores(
                h * chunks + t, [None] * t + [row <= col],
                q_copy(h).wait if t == 0 else None,
            )
            for h in range(heads)
            for t in range(chunks)
        ]
        + [
            own_scores(
                last, [row + c * BLK < reach for c in range(chunks)],
                functools.partial(tails_in, q_hbm, q_s, qb_sem),
            )
        ]
    )

    kb_copy.wait()
    vb_copy.wait()
    for step in range(1, n):
        for copy in kv_copies(step):
            copy.wait()
    kbt_s[...] = kb_s[...].T
    vbt_s[...] = vb_s[...].T
    ones = jnp.ones((8, HD), bf16)

    def beacon_part(b, bias, live_rows, wait=None, done=None):
        if wait is not None:
            wait()
        query = q_s[block_rows(b), :]
        grad = g_s[block_rows(b), :]
        if live_rows is not None:
            grad = jnp.where(live_rows, grad.astype(f32), 0.0).astype(bf16)
            g_s[block_rows(b), :] = grad
        scores = nt(kb_s[...], query) + bias[...]
        yield
        own_top = stat_s[b, 0:1, :]
        top = jnp.maximum(own_top, jnp.max(scores, axis=0, keepdims=True))
        e = jnp.exp2((scores - top) * SCALE_LOG2E)
        shrink = jnp.exp2((own_top - top) * SCALE_LOG2E)
        total = shrink * stat_s[b, 1:2, :] + jnp.sum(e, axis=0, keepdims=True)
        inverse = 1.0 / total
        factor = shrink * inverse
        probs = e * inverse
        weights = probs.astype(bf16)
        yield
        out = (ot_s[b] * factor + nn(vbt_s[...], weights)).T
        if live_rows is not None:
            out = jnp.where(live_rows, out, 0.0)
        out = out.astype(bf16)
        o_s[block_rows(b), :] = out
        if done is not None:
            done()
        yield
        terms = grad.astype(f32) * out.astype(f32)
        high = terms.astype(bf16)
        low = (terms - high.astype(f32)).astype(bf16)
        delta = (nt(ones, high) + nt(ones, low))[0:1, :]
        slope = nt(vb_s[...], grad)
        yield
        sgrad = (probs * (slope - delta)).astype(bf16)
        yield
        term_s[:, 0:HD] += nn(sgrad, query)
        term_s[:, HD : 2 * HD] += nn(weights, grad)
        ot_s[b] = nn(kbt_s[...], sgrad)
        stat_s[b, 0:1, :] = factor
        stat_s[b, 1:2, :] = delta

    def o_copy(h):
        return pltpu.make_async_copy(
            o_s.at[head_rows(h)], o_hbm.at[pl.ds(0, SPAN), head_cols(h)], o_sem.at[h]
        )

    def dq_copy(h):
        return pltpu.make_async_copy(
            dq_s.at[head_rows(h)], dq_hbm.at[pl.ds(0, SPAN), head_cols(h)], dq_sem.at[h]
        )

    def tail_out(src, dst, sem, h):
        return pltpu.make_async_copy(
            src.at[pl.ds(last * BLK + h * BMAX, BMAX)],
            dst.at[pl.ds(SPAN, BMAX), pl.ds(h * HD, HD)],
            sem.at[h],
        )

    def tails_out(src, dst, sem):
        for h in range(heads):
            tail_out(src, dst, sem, h).start()

    row_slot = lax.rem(lax.broadcasted_iota(jnp.int32, (BLK, HD), 0), BMAX)
    interleave(
        [
            beacon_part(
                h * chunks + t, bias_s, None,
                g_copy(h).wait if t == 0 else None,
                o_copy(h).start if t == chunks - 1 else None,
            )
            for h in range(heads)
            for t in range(chunks)
        ]
        + [
            beacon_part(
                last, bbias_s, (row_slot + 1) * own_ratio <= SPAN,
                functools.partial(tails_in, g_hbm, g_s, gb_sem),
                functools.partial(tails_out, o_s, o_hbm, ob_sem),
            )
        ]
    )

    def own_part(b, count, done=None):
        query = q_s[block_rows(b), :]
        grad = g_s[block_rows(b), :]
        factor = stat_s[b, 0:1, :]
        delta = stat_s[b, 1:2, :]
        keys = pl.ds(0, count * BLK)
        slope = nt(v_s[keys, :], grad)
        yield
        probs = e_s[b, keys, :].astype(f32) * factor
        sgrad = (probs * (slope - delta)).astype(bf16)
        yield
        dk_s[keys, :] += nn(sgrad, query)
        dv_s[keys, :] += nn(probs.astype(bf16), grad)
        dqt = ot_s[b] + nn(kt_s[:, keys], sgrad)
        yield
        dq_s[block_rows(b), :] = (dqt * SCALE).T.astype(bf16)
        if done is not None:
            done()

    def term_copy(step):
        peer = lax.rem(me + step, n)
        return pltpu.make_async_remote_copy(
            src_ref=term_s.at[pl.ds(pl.multiple_of(peer * BMAX, BMAX), BMAX)],
            dst_ref=recv_s.at[step - 1],
            send_sem=term_send.at[step - 1], recv_sem=term_recv.at[step - 1],
            device_id={"span": peer}, device_id_type=pl.DeviceIdType.MESH,
        )

    interleave(
        [own_part(last, chunks, functools.partial(tails_out, dq_s, dq_hbm, dqb_sem))]
    )
    for step in range(1, n):
        term_copy(step).start()

    interleave(
        [
            own_part(
                h * chunks + t, t + 1, dq_copy(h).start if t == chunks - 1 else None
            )
            for h in range(heads)
            for t in range(chunks)
        ]
    )

    dk_out[0:SPAN, :] = (dk_s[...] * SCALE).astype(bf16)
    dv_out[0:SPAN, :] = dv_s[...].astype(bf16)
    total = term_s[mine, :]
    for step in range(1, n):
        term_copy(step).wait()
        total = total + recv_s[step - 1]
    dk_out[SPAN : SPAN + BMAX, :] = (total[:, 0:HD] * SCALE).astype(bf16)
    dv_out[SPAN : SPAN + BMAX, :] = total[:, HD : 2 * HD].astype(bf16)

    for h in range(heads):
        o_copy(h).wait()
        dq_copy(h).wait()
        tail_out(o_s, o_hbm, ob_sem, h).wait()
        tail_out(dq_s, dq_hbm, dqb_sem, h).wait()


def local(n, query_rows, key_rows, value_rows, out_grad, ratios):
    heads = query_rows.shape[1] // HD
    chunks = SPAN // BLK
    blocks = heads * chunks + 1
    nb = n * BMAX
    any_spec = pl.BlockSpec(memory_space=pltpu.HBM)
    vmem_spec = pl.BlockSpec(memory_space=pltpu.VMEM)
    dma = pltpu.SemaphoreType.DMA
    return pl.pallas_call(
        functools.partial(kernel, n, heads),
        out_shape=(
            jax.ShapeDtypeStruct(query_rows.shape, bf16),
            jax.ShapeDtypeStruct(query_rows.shape, bf16),
            jax.ShapeDtypeStruct(key_rows.shape, bf16),
            jax.ShapeDtypeStruct(value_rows.shape, bf16),
        ),
        in_specs=[pl.BlockSpec(memory_space=pltpu.SMEM)] + [any_spec] * 4,
        out_specs=(pl.BlockSpec(memory_space=pl.ANY), pl.BlockSpec(memory_space=pl.ANY), vmem_spec, vmem_spec),
        scratch_shapes=[
            pltpu.VMEM((blocks * BLK, HD), bf16),
            pltpu.VMEM((blocks * BLK, HD), bf16),
            pltpu.VMEM((SPAN, HD), bf16),
            pltpu.VMEM((SPAN, HD), bf16),
            pltpu.VMEM((HD, SPAN), bf16),
            pltpu.VMEM((HD, SPAN), bf16),
            pltpu.VMEM((nb, HD), bf16),
            pltpu.VMEM((nb, HD), bf16),
            pltpu.VMEM((HD, nb), bf16),
            pltpu.VMEM((HD, nb), bf16),
            pltpu.VMEM((blocks, SPAN, BLK), bf16),
            pltpu.VMEM((blocks, HD, BLK), f32),
            pltpu.VMEM((blocks, 8, BLK), f32),
            pltpu.VMEM((nb, BLK), f32),
            pltpu.VMEM((nb, BLK), f32),
            pltpu.VMEM((nb, 2 * HD), f32),
            pltpu.VMEM((n - 1, BMAX, 2 * HD), f32),
            pltpu.VMEM((SPAN, HD), f32),
            pltpu.VMEM((SPAN, HD), f32),
            pltpu.VMEM((blocks * BLK, HD), bf16),
            pltpu.VMEM((blocks * BLK, HD), bf16),
            dma((4,)), dma((heads,)), dma((heads,)), dma((heads,)), dma((heads,)),
            dma((heads,)), dma((heads,)), dma((heads,)), dma((heads,)),
            dma((2, n - 1)), dma((2, n - 1)), dma((n - 1,)), dma((n - 1,)),
        ],
        compiler_params=pltpu.CompilerParams(
            collective_id=0, has_side_effects=True, vmem_limit_bytes=67043328
        ),
        name="beacon_attention",
    )(ratios, query_rows, key_rows, value_rows, out_grad)


def solution(mesh):
    rows = P(("seq", "span"), "kvg")
    return jax.shard_map(
        functools.partial(local, mesh.shape["span"]),
        mesh=mesh,
        in_specs=(rows, rows, rows, rows, P("seq")),
        out_specs=(rows, rows, rows, rows),
        check_vma=False,
    )
```

profile of v0, /device:TPU:0, one launch (start us, length us, event | category | flops | bytes accessed | tf_op | source)
XLA Modules:
  0.0 25.9 jit_solution(14202522102109519323)
XLA Ops:
  0.6 20.3 %beacon_attention.1 = (bf16[544,896]{1,0:T(8,128)(2,1)}, bf16[544,896]{1,0:T(8,128)(2,1)}, bf16[544,128]{1,0:T(8,128)(2,1)}, bf16[544,128]{1,0:T(8,128)(2,1)}) custom-call(s32[4]{0:T(128)} %ratios_ref.1, bf16[544,896]{1,0:T(8,128)(2,1)} %q_hbm.1, bf16[544,128]{1,0:T(8,128)(2,1)} %k_hbm.1, bf16[544,128]{1,0:T(8,128)(2,1)} %v_hbm.1, bf16[544,896]{1,0:T(8,128)(2,1)} %g_hbm.1), custom_call_target="tpu_custom_call" | custom-call | tf_op jit(solution)/shard_map/beacon_attention/pallas_call | solution.py:367
  20.9 0.0 copy-start
  20.9 2.3 %copy.13 = bf16[544,896]{1,0:T(8,128)(2,1)} copy(bf16[544,896]{1,0:T(8,128)(2,1)} %get-tuple-element.8) | data formatting | bytes 1949696
  23.2 0.0 copy-done
  23.2 0.0 copy-start.2
  23.2 0.9 %copy.14 = bf16[544,896]{1,0:T(8,128)(2,1)} copy(bf16[544,896]{1,0:T(8,128)(2,1)S(1)} %copy-done) | data formatting | bytes 1949696
  24.2 0.1 copy-done.2
  24.3 0.0 copy-start.1
  24.3 0.7 %copy.15 = bf16[544,128]{1,0:T(8,128)(2,1)} copy(bf16[544,128]{1,0:T(8,128)(2,1)S(1)} %copy-done.2) | data formatting | bytes 278528
  24.9 0.3 %copy-done.1 = bf16[544,128]{1,0:T(8,128)(2,1)S(1)} copy-done((bf16[544,128]{1,0:T(8,128)(2,1)S(1)}, bf16[544,128]{1,0:T(8,128)(2,1)}, u32[]{:S(2)}) %copy-start.1) | copy-done | bytes 139288
  25.2 0.7 %copy.16 = bf16[544,128]{1,0:T(8,128)(2,1)} copy(bf16[544,128]{1,0:T(8,128)(2,1)S(1)} %copy-done.1) | data formatting | bytes 278528
Async XLA Ops:
  20.9 2.3 %copy-start = (bf16[544,896]{1,0:T(8,128)(2,1)S(1)}, bf16[544,896]{1,0:T(8,128)(2,1)}, u32[]{:S(2)}) copy-start(bf16[544,896]{1,0:T(8,128)(2,1)} %get-tuple-element.9) | copy-start | bytes 2924548
  23.2 1.0 %copy-start.2 = (bf16[544,128]{1,0:T(8,128)(2,1)S(1)}, bf16[544,128]{1,0:T(8,128)(2,1)}, u32[]{:S(2)}) copy-start(bf16[544,128]{1,0:T(8,128)(2,1)} %get-tuple-element.10) | copy-start | bytes 417796
  24.3 1.0 %copy-start.1 = (bf16[544,128]{1,0:T(8,128)(2,1)S(1)}, bf16[544,128]{1,0:T(8,128)(2,1)}, u32[]{:S(2)}) copy-start(bf16[544,128]{1,0:T(8,128)(2,1)} %get-tuple-element.11) | copy-start | bytes 417796
where the time goes:
time: 26.1 us; the launch traced here: 25.9 us
  Pallas kernels  20.3 us (78%)
  local copies, waits for them, and re-layouts  4.95 us (19%)
  between operations  0.65 us (2%)
    pallas_call x1, Pallas kernels, local(): pl.pallas_call(functools.partial(kernel, n, heads), out_shape=(jax.ShapeD...  20.3 us
    unnamed x10, local copies, waits for them, and re-layouts  4.95 us

commit v1 on v0

v1 whole, which is shorter than its diff:
```python
import functools
import math

import jax
import jax.numpy as jnp
from jax import lax
from jax.experimental import pallas as pl
from jax.experimental.pallas import tpu as pltpu
from jax.sharding import PartitionSpec as P

SPAN = 512
HD = 128
BMAX = 32
BLK = 256
SUB = 128

SCALE = HD ** (-0.5)
SCALE_LOG2E = SCALE * math.log2(math.e)
FLOOR = -1e30

f32 = jnp.float32
bf16 = jnp.bfloat16


def nt(a, b):
    return lax.dot_general(a, b, (((1,), (1,)), ((), ())), preferred_element_type=f32)


def nn(a, b):
    return lax.dot_general(a, b, (((1,), (0,)), ((), ())), preferred_element_type=f32)


def interleave(blocks):
    waiting, active = list(blocks), []
    while waiting or active:
        if waiting:
            active.append(waiting.pop(0))
        active = [block for block in active if next(block, "end") != "end"]


def fold(op, x, rows=32):
    out = x[0:rows]
    for i in range(rows, x.shape[0], rows):
        out = op(out, x[i : i + rows])
    return out


def plan(heads):
    blocks = []
    for t in range(SPAN // SUB):
        for h in range(0, heads - 1, 2):
            blocks.append((h, 2, t * SUB, SUB, (t + 1) * SUB))
        if heads % 2 and t % 2:
            blocks.append((heads - 1, 1, (t - 1) * SUB, BLK, (t + 1) * SUB))
    return blocks


def kernel(
    n, heads,
    ratios_hbm, q_hbm, k_hbm, v_hbm, g_hbm,
    o_s, dq_s, dk_out, dv_out,
    q_s, g_s, k_s, v_s, kt_s, vt_s, kv_s, kbt_s, vbt_s,
    s_s, sl_s, e_s, sg_s, pb_s, sb_s, qt_s, gt_s, stat_s, bias_s, bbias_s, pair_s, single_s,
    term_s, send_s, recv_s, dk_s, dv_s,
    ratios_ref, ratio_sem, in_sem, q_sem, g_sem, kv_send, kv_recv, term_send, term_recv,
):
    me = lax.axis_index("span")
    nb = n * BMAX
    seen = (n - 1) * BMAX
    bands = SPAN // SUB
    blocks = plan(heads)
    last = len(blocks)
    mine = pl.ds(pl.multiple_of(me * BMAX, BMAX), BMAX)
    left, right = pl.ds(0, HD), pl.ds(HD, HD)

    ratio_copy = pltpu.make_async_copy(ratios_hbm, ratios_ref, ratio_sem)
    k_copy = pltpu.make_async_copy(k_hbm.at[pl.ds(0, SPAN)], k_s, in_sem.at[0])
    v_copy = pltpu.make_async_copy(v_hbm.at[pl.ds(0, SPAN)], v_s, in_sem.at[1])
    kb_copy = pltpu.make_async_copy(
        k_hbm.at[pl.ds(SPAN, BMAX)], kv_s.at[mine, left], in_sem.at[2]
    )
    vb_copy = pltpu.make_async_copy(
        v_hbm.at[pl.ds(SPAN, BMAX)], kv_s.at[mine, right], in_sem.at[3]
    )

    def band_copy(src, dst, sem, t):
        rows = pl.ds(t * SUB, SUB if t < bands else BMAX)
        return pltpu.make_async_copy(src.at[rows], dst.at[rows], sem.at[t])

    kv_s[...] = jnp.zeros_like(kv_s)
    barrier = pltpu.get_barrier_semaphore()
    for step in range(1, n):
        @pl.when(me >= step)
        def _():
            pl.semaphore_signal(
                barrier, inc=1, device_id={"span": me - step},
                device_id_type=pl.DeviceIdType.MESH,
            )

    k_copy.start()
    band_copy(q_hbm, q_s, q_sem, 0).start()
    v_copy.start()
    band_copy(g_hbm, g_s, g_sem, 0).start()
    ratio_copy.start()

    recv_s[...] = jnp.zeros_like(recv_s)

    kb_copy.start()
    vb_copy.start()
    for t in range(1, bands + 1):
        band_copy(q_hbm, q_s, q_sem, t).start()
        band_copy(g_hbm, g_s, g_sem, t).start()

    term_s[...] = jnp.zeros_like(term_s)
    dk_s[...] = jnp.zeros_like(dk_s)
    dv_s[...] = jnp.zeros_like(dv_s)
    for b in range(last):
        for ref in (pb_s, sb_s):
            ref[b, pl.ds(seen, BMAX), :] = jnp.zeros((BMAX, BLK), bf16)
    row = lax.broadcasted_iota(jnp.int32, (BLK, BLK), 0)
    col = lax.broadcasted_iota(jnp.int32, (BLK, BLK), 1)
    single_s[...] = jnp.where(row <= col, 0.0, FLOOR)
    pair_s[...] = jnp.where(row <= lax.rem(col, SUB), 0.0, FLOOR)[0:SUB]

    ratio_copy.wait()
    own_ratio = ratios_ref[me]
    key_id = lax.broadcasted_iota(jnp.int32, (nb, BLK), 0)
    lane_slot = lax.rem(lax.broadcasted_iota(jnp.int32, (nb, BLK), 1), BMAX)
    key_slot = lax.rem(key_id, BMAX)
    key_span = key_id // BMAX
    key_ratio = jnp.zeros((nb, BLK), jnp.int32)
    for s in range(n):
        key_ratio = jnp.where(key_span == s, ratios_ref[s], key_ratio)
    live = (key_slot + 1) * key_ratio <= SPAN
    before = live & (key_span < me)
    bias_s[...] = jnp.where(before, 0.0, FLOOR)
    bbias_s[...] = jnp.where(
        before | (live & (key_span == me) & (key_slot <= lane_slot)), 0.0, FLOOR
    )
    reach = (lax.rem(lax.broadcasted_iota(jnp.int32, (SUB, BLK), 1), BMAX) + 1) * own_ratio
    sub_row = lax.broadcasted_iota(jnp.int32, (SUB, BLK), 0)
    row_live = (lax.broadcasted_iota(jnp.int32, (BMAX, HD), 0) + 1) * own_ratio <= SPAN
    lane_live = (
        lax.rem(lax.broadcasted_iota(jnp.int32, (1, BLK), 1), BMAX) + 1
    ) * own_ratio <= SPAN

    def kv_copy(step):
        return pltpu.make_async_remote_copy(
            src_ref=kv_s.at[mine], dst_ref=kv_s.at[mine],
            send_sem=kv_send.at[step - 1], recv_sem=kv_recv.at[step - 1],
            device_id={"span": lax.rem(me + step, n)}, device_id_type=pl.DeviceIdType.MESH,
        )

    def send_kv(first, part):
        @pl.when(me == 0 if first else (me > 0) & (me < n - 1))
        def _():
            if part == 0:
                pl.semaphore_wait(barrier, n - 1 - me)
            for step in range(n - 1, 0, -1):
                @pl.when(me + step == n - 1 if part == 0 else me + step < n - 1)
                def _():
                    kv_copy(step).start()

    def wait_kv(first):
        for step in range(1, n):
            @pl.when(me == step if first else me > step)
            def _():
                kv_copy(step).wait_recv()

    def call(*functions):
        for function in functions:
            function()
        yield

    def load(ref, b):
        if b == last:
            tail = pl.ds(SPAN, BMAX)
            parts = [ref[tail, pl.ds(h * HD, HD)] for h in range(heads)]
            parts.append(jnp.zeros((BLK - heads * BMAX, HD), bf16))
        else:
            h, count, start, size, _ = blocks[b]
            parts = [
                ref[pl.ds(start, size), pl.ds((h + i) * HD, HD)] for i in range(count)
            ]
        return jnp.concatenate(parts, 0)

    def scatter(ref, b, value):
        if b == last:
            for h in range(heads):
                ref[pl.ds(SPAN, BMAX), pl.ds(h * HD, HD)] = value[h * BMAX : (h + 1) * BMAX]
        else:
            h, count, start, size, _ = blocks[b]
            for i in range(count):
                ref[pl.ds(start, size), pl.ds((h + i) * HD, HD)] = value[
                    i * size : (i + 1) * size
                ]

    def keys_of(b):
        return SPAN if b == last else blocks[b][4]

    def own_scores(b, wait):
        wait()
        if b == last:
            for h in range(heads):
                spot = (pl.ds(SPAN, BMAX), pl.ds(h * HD, HD))
                g_s[spot] = jnp.where(row_live, g_s[spot].astype(f32), 0.0).astype(bf16)
        keys = keys_of(b)
        scores = nt(k_s[pl.ds(0, keys), :], load(q_s, b))
        top = None
        for c in range(0, keys, SUB):
            part = scores[c : c + SUB]
            if b == last:
                part = jnp.where(sub_row + c < reach, part, FLOOR)
            elif blocks[b][1] == 2 and c == keys - SUB:
                part = part + pair_s[...]
            elif blocks[b][1] == 1 and c >= keys - BLK:
                at = c - (keys - BLK)
                part = part + single_s[at : at + SUB, :]
            s_s[b, pl.ds(c, SUB), :] = part
            part = fold(jnp.maximum, part)
            top = part if top is None else jnp.maximum(top, part)
        qt_s[b] = load(q_s, b).T
        yield
        slope = nt(v_s[pl.ds(0, keys), :], load(g_s, b))
        gt_s[b] = load(g_s, b).T
        sl_s[b, pl.ds(0, keys), :] = slope
        top = jnp.max(top, axis=0, keepdims=True)
        stat_s[b, 0:1, :] = top
        yield
        total = dot = None
        for c in range(0, keys, SUB):
            e = jnp.exp2((s_s[b, pl.ds(c, SUB), :] - top) * SCALE_LOG2E)
            e_s[b, pl.ds(c, SUB), :] = e.astype(bf16)
            part = fold(jnp.add, e)
            total = part if total is None else total + part
            part = fold(jnp.add, e * sl_s[b, pl.ds(c, SUB), :])
            dot = part if dot is None else dot + part
        stat_s[b, 1:2, :] = jnp.sum(total, axis=0, keepdims=True)
        stat_s[b, 2:3, :] = jnp.sum(dot, axis=0, keepdims=True)

    def band_waits(t):
        def run():
            band_copy(q_hbm, q_s, q_sem, t).wait()
            band_copy(g_hbm, g_s, g_sem, t).wait()
        return run

    waits, t = [], 0
    for h, count, start, size, _ in blocks:
        need = (start + size) // SUB - 1
        waits.append(band_waits(need) if need >= t else lambda: None)
        t = max(t, need + 1)
    waits.append(band_waits(bands))

    k_copy.wait()
    v_copy.wait()

    def beacon_early(b):
        count = nb if b == last else seen
        used = pl.ds(BMAX, count - BMAX)
        bias = bbias_s if b == last else bias_s
        scores = nn(kv_s[used, left], qt_s[b]) + bias[used, :]
        slope = nn(kv_s[used, right], gt_s[b])
        top = fold(jnp.maximum, scores)
        yield
        own_top = stat_s[b, 0:1, :]
        top = jnp.maximum(own_top, jnp.max(top, axis=0, keepdims=True))
        e = jnp.exp2((scores - top) * SCALE_LOG2E)
        shrink = jnp.exp2((own_top - top) * SCALE_LOG2E)
        pb_s[b, used, :] = e.astype(bf16)
        total = jnp.sum(fold(jnp.add, e), axis=0, keepdims=True)
        dot = jnp.sum(fold(jnp.add, e * slope), axis=0, keepdims=True)
        stat_s[b, 0:1, :] = top
        stat_s[b, 1:2, :] = shrink * stat_s[b, 1:2, :] + total
        stat_s[b, 2:3, :] = shrink * stat_s[b, 2:3, :] + dot
        stat_s[b, 3:4, :] = shrink

    def beacon_late(b):
        late = pl.ds(0, BMAX)
        bias = bbias_s if b == last else bias_s
        scores = nn(kv_s[late, left], qt_s[b]) + bias[late, :]
        slope = nn(kv_s[late, right], gt_s[b])
        yield
        old_top = stat_s[b, 0:1, :]
        top = jnp.maximum(old_top, jnp.max(scores, axis=0, keepdims=True))
        e = jnp.exp2((scores - top) * SCALE_LOG2E)
        shrink = jnp.exp2((old_top - top) * SCALE_LOG2E)
        total = shrink * stat_s[b, 1:2, :] + jnp.sum(e, axis=0, keepdims=True)
        dot = shrink * stat_s[b, 2:3, :] + jnp.sum(e * slope, axis=0, keepdims=True)
        inverse = 1.0 / total
        shrink = shrink * inverse
        delta = inverse * dot
        if b == last:
            delta = jnp.where(lane_live, delta, 0.0)
        stat_s[b, 3:4, :] = shrink * stat_s[b, 3:4, :]
        stat_s[b, 4:5, :] = delta
        stat_s[b, 5:6, :] = shrink
        yield
        probs = e * inverse
        pb_s[b, late, :] = probs.astype(bf16)
        sb_s[b, late, :] = (probs * (slope - delta)).astype(bf16)

    def beacon_rest(b):
        used = pl.ds(BMAX, (nb if b == last else seen) - BMAX)
        slope = nn(kv_s[used, right], gt_s[b])
        probs = pb_s[b, used, :].astype(f32) * stat_s[b, 5:6, :]
        pb_s[b, used, :] = probs.astype(bf16)
        yield
        sb_s[b, used, :] = (probs * (slope - stat_s[b, 4:5, :])).astype(bf16)

    def term_part(members, used):
        for ref, rows, cols in ((pb_s, g_s, right), (sb_s, q_s, left)):
            term_s[used, cols] += nn(
                jnp.concatenate([ref[b, used, :] for b in members], 1),
                jnp.concatenate([load(rows, b) for b in members], 0),
            )
            yield

    def with_terms(part, size, used_of):
        order, ready = [], None
        for at in range(0, last + 1, size):
            members = list(range(at, min(at + size, last + 1)))
            order += [part(b) for b in members]
            if ready:
                order.append(term_part(ready, used_of(ready)))
            ready = members
        return order + [call(), term_part(ready, used_of(ready))]

    order = [own_scores(b, waits[b]) for b in range(last + 1)]
    order.insert(14 + 1, call(lambda: send_kv(True, 1)))
    order.insert(14, call(lambda: send_kv(True, 0)))
    order.insert(3 + 1, call(lambda: send_kv(False, 1)))
    order.insert(3, call(kb_copy.wait, vb_copy.wait, lambda: send_kv(False, 0)))
    order.append(call(lambda: wait_kv(False)))
    order += [beacon_early(b) for b in range(last + 1)]
    order.append(call(lambda: wait_kv(True)))
    interleave(order + with_terms(beacon_late, 4, lambda members: pl.ds(0, BMAX)))

    def term_copy(step):
        peer = lax.rem(me + (n - step), n)
        return pltpu.make_async_remote_copy(
            src_ref=send_s.at[pl.ds(pl.multiple_of(peer * BMAX, BMAX), BMAX)],
            dst_ref=recv_s.at[step - 1],
            send_sem=term_send.at[step - 1], recv_sem=term_recv.at[step - 1],
            device_id={"span": peer}, device_id_type=pl.DeviceIdType.MESH,
        )

    def send_terms(first):
        rows = pl.ds(0, BMAX) if first else pl.ds(BMAX, nb - BMAX)
        send_s[rows, :] = term_s[rows, :].astype(bf16)
        for step in range(n - 1, 0, -1):
            @pl.when(me == step if first else me > step)
            def _():
                term_copy(step).start()

    send_terms(True)
    kt_s[...] = k_s[...].T
    vt_s[...] = v_s[...].T
    kbt_s[...] = kv_s[:, left].T
    vbt_s[...] = kv_s[:, right].T

    def own_part(b):
        keys = keys_of(b)
        delta = stat_s[b, 4:5, :]
        half = stat_s[b, 3:4, :].astype(bf16)
        for c in range(0, keys, SUB):
            spot = pl.ds(c, SUB)
            probs = e_s[b, spot, :] * half
            e_s[b, spot, :] = probs
            sg_s[b, spot, :] = (sl_s[b, spot, :] - delta).astype(bf16) * probs
        yield
        out = nn(
            jnp.concatenate([vt_s[:, pl.ds(0, keys)], vbt_s[...]], 1),
            jnp.concatenate([e_s[b, pl.ds(0, keys), :], pb_s[b]], 0),
        )
        if b == last:
            out = jnp.where(lane_live, out, 0.0)
        scatter(o_s, b, out.astype(bf16).T)
        yield
        dqt = nn(
            jnp.concatenate([kt_s[:, pl.ds(0, keys)], kbt_s[...]], 1),
            jnp.concatenate([sg_s[b, pl.ds(0, keys), :], sb_s[b]], 0),
        )
        scatter(dq_s, b, (dqt * SCALE).astype(bf16).T)
        yield
        used = pl.ds(0, keys)
        dk_s[used, :] += nn(sg_s[b, used, :], load(q_s, b))
        yield
        dv_s[used, :] += nn(e_s[b, used, :], load(g_s, b))

    def used_rest(members):
        return pl.ds(BMAX, (nb if last in members else seen) - BMAX)

    order = with_terms(beacon_rest, 2, used_rest)
    order += [own_part(0), own_part(1), own_part(2), call(lambda: send_terms(False))]
    interleave(order + [own_part(b) for b in range(3, last + 1)])

    dk_out[0:SPAN, :] = (dk_s[...] * SCALE).astype(bf16)
    dv_out[0:SPAN, :] = dv_s[...].astype(bf16)
    for step in range(1, n):
        @pl.when(me + step < n)
        def _():
            term_copy(step).wait_recv()
    total = term_s[mine, :]
    for step in range(1, n):
        total = total + recv_s[step - 1].astype(f32)
    dk_out[SPAN : SPAN + BMAX, :] = (total[:, 0:HD] * SCALE).astype(bf16)
    dv_out[SPAN : SPAN + BMAX, :] = total[:, HD : 2 * HD].astype(bf16)
    for step in range(1, n):
        @pl.when(me + step < n)
        def _():
            kv_copy(step).wait_send()
        @pl.when(me >= step)
        def _():
            term_copy(step).wait_send()


def write_kernel(o_s, dq_s, dk_s, dv_s, o_hbm, dq_hbm, dk_hbm, dv_hbm, sem):
    pairs = ((o_s, o_hbm), (dq_s, dq_hbm), (dk_s, dk_hbm), (dv_s, dv_hbm))
    copies = [
        pltpu.make_async_copy(src, dst, sem.at[i]) for i, (src, dst) in enumerate(pairs)
    ]
    for copy in copies:
        copy.start()
    for copy in copies:
        copy.wait()


def local(n, query_rows, key_rows, value_rows, out_grad, ratios):
    heads = query_rows.shape[1] // HD
    blocks = len(plan(heads)) + 1
    rows = query_rows.shape[0]
    bands = SPAN // SUB + 1
    nb = n * BMAX
    any_spec = pl.BlockSpec(memory_space=pltpu.HBM)
    vmem_spec = pl.BlockSpec(memory_space=pltpu.VMEM)
    dma = pltpu.SemaphoreType.DMA
    vmem = pltpu.VMEM
    args = [
        pltpu.with_memory_space_constraint(x, pltpu.HBM)
        for x in (ratios, query_rows, key_rows, value_rows, out_grad)
    ]
    parts = pl.pallas_call(
        functools.partial(kernel, n, heads),
        out_shape=(
            vmem(query_rows.shape, bf16),
            vmem(query_rows.shape, bf16),
            vmem(key_rows.shape, bf16),
            vmem(value_rows.shape, bf16),
        ),
        in_specs=[any_spec] * 5,
        out_specs=(vmem_spec,) * 4,
        scratch_shapes=[
            vmem(query_rows.shape, bf16),
            vmem(query_rows.shape, bf16),
            vmem((SPAN, HD), bf16),
            vmem((SPAN, HD), bf16),
            vmem((HD, SPAN), bf16),
            vmem((HD, SPAN), bf16),
            vmem((nb, 2 * HD), bf16),
            vmem((HD, nb), bf16),
            vmem((HD, nb), bf16),
            vmem((blocks, SPAN, BLK), f32),
            vmem((blocks, SPAN, BLK), f32),
            vmem((blocks, SPAN, BLK), bf16),
            vmem((blocks, SPAN, BLK), bf16),
            vmem((blocks, nb, BLK), bf16),
            vmem((blocks, nb, BLK), bf16),
            vmem((blocks, HD, BLK), bf16),
            vmem((blocks, HD, BLK), bf16),
            vmem((blocks, 8, BLK), f32),
            vmem((nb, BLK), f32),
            vmem((nb, BLK), f32),
            vmem((SUB, BLK), f32),
            vmem((BLK, BLK), f32),
            vmem((nb, 2 * HD), f32),
            vmem((nb, 2 * HD), bf16),
            vmem((n - 1, BMAX, 2 * HD), bf16),
            vmem((SPAN, HD), f32),
            vmem((SPAN, HD), f32),
            pltpu.SMEM((n,), jnp.int32), dma(()), dma((4,)), dma((bands,)), dma((bands,)),
            dma((n - 1,)), dma((n - 1,)), dma((n - 1,)), dma((n - 1,)),
        ],
        compiler_params=pltpu.CompilerParams(
            collective_id=0, has_side_effects=True, vmem_limit_bytes=60 << 20
        ),
        name="beacon_attention",
    )(*args)
    parts = [pltpu.with_memory_space_constraint(part, pltpu.VMEM) for part in parts]
    return pl.pallas_call(
        write_kernel,
        out_shape=(
            jax.ShapeDtypeStruct(query_rows.shape, bf16),
            jax.ShapeDtypeStruct(query_rows.shape, bf16),
            jax.ShapeDtypeStruct(key_rows.shape, bf16),
            jax.ShapeDtypeStruct(value_rows.shape, bf16),
        ),
        in_specs=[vmem_spec] * 4,
        out_specs=(any_spec,) * 4,
        scratch_shapes=[dma((4,))],
        name="write_rows",
    )(*parts)


def solution(mesh):
    rows = P(("seq", "span"), "kvg")
    return jax.shard_map(
        functools.partial(local, mesh.shape["span"]),
        mesh=mesh,
        in_specs=(rows, rows, rows, rows, P("seq")),
        out_specs=(rows, rows, rows, rows),
        check_vma=False,
    )
```

time: 26.1 us -> 15.8 us (0.61)
  Pallas kernels: 20.3 us -> 15 us
  local copies, waits for them, and re-layouts: 4.95 us -> 0 us
    pallas_call x1 -> x2, Pallas kernels: 20.3 us -> 15 us  [the longest x1 13.6 us: local(): pl.pallas_call(functools.partial(kernel, n, heads), out_shape=(vmem(query...]
    unnamed x10 -> x0, local copies, waits for them, and re-layouts: 4.95 us -> none
where the time goes in v1:
time: 15.8 us; the launch traced here: 15.7 us
  Pallas kernels  15 us (95%)
  between operations  0.64 us (4%)
    pallas_call x1, Pallas kernels, local(): pl.pallas_call(functools.partial(kernel, n, heads), out_shape=(vmem(query...  13.6 us
    pallas_call x1, Pallas kernels, local(): pl.pallas_call(write_kernel, out_shape=(jax.ShapeDtypeStruct(query_rows.s...  1.38 us

profile of v1, /device:TPU:0, one launch (start us, length us, event | category | flops | bytes accessed | tf_op | source)
XLA Modules:
  0.0 15.7 jit_solution(15781599868789668779)
XLA Ops:
  0.6 13.6 %beacon_attention.1 = (bf16[544,896]{1,0:T(8,128)(2,1)S(1)}, bf16[544,896]{1,0:T(8,128)(2,1)S(1)}, bf16[544,128]{1,0:T(8,128)(2,1)S(1)}, bf16[544,128]{1,0:T(8,128)(2,1)S(1)}) custom-call(s32[4]{0:T(128)} %ratios_hbm.1, bf16[544,896]{1,0:T(8,128)(2,1)} %q_hbm.1, bf16[544,128]{1,0:T(8,128)(2,1)} %k_hbm.1, bf16[544,128]{1,0:T(8,128)(2,1)} %v_hbm.1, ...), custom_call_target="tpu_custom_call" | custom-call | tf_op jit(solution)/shard_map/beacon_attention/pallas_call | solution.py:442
  14.3 1.4 %write_rows.1 = (bf16[544,896]{1,0:T(8,128)(2,1)}, bf16[544,896]{1,0:T(8,128)(2,1)}, bf16[544,128]{1,0:T(8,128)(2,1)}, bf16[544,128]{1,0:T(8,128)(2,1)}) custom-call(bf16[544,896]{1,0:T(8,128)(2,1)S(1)} %get-tuple-element.8.o_s, bf16[544,896]{1,0:T(8,128)(2,1)S(1)} %get-tuple-element.9.dq_s, bf16[544,128]{1,0:T(8,128)(2,1)S(1)} %get-tuple-element.10.dk_s, ...), custom_call_target="tpu_custom_call" | custom-call | tf_op jit(solution)/shard_map/write_rows/pallas_call | solution.py:489
